TPU v7x, 128 devices: a whole 4x4x4 slice. The times are simulated.
128 devices in a mesh: row: 8 (over z, core), col: 16 (over y, x).
Axes of the slice: x: 4, y: 4, z: 4, core: 2. Of those that a mesh axis runs over, the one named last changes fastest.
Arguments:
- hidden: bfloat16 [1408, 16384], P('col', 'row'), may hold values from -18 to 18
- gain_in: bfloat16 [1408], replicated, may hold values from 0.5 to 1.5
- w_query: bfloat16 [1408, 1408], P('col'), may hold values from -0.3125 to 0.3125
- w_pair: bfloat16 [2, 1408, 1408], P(None, 'col'), may hold values from -0.15625 to 0.15625
- kv_cache: bfloat16 [2, 1408, 16384], P(None, 'col', 'row'), may hold values from -103 to 103
- recompute_rows: int32 [8, 200], P('row'), may hold values from 0 to 2047, as said below
- segment_ids: int32 [16384], P('row'), may hold values from -1 to 1, as said below
- w_out: bfloat16 [1408, 1408], P('col'), may hold values from -0.3125 to 0.3125
- gain_merge: bfloat16 [1408], replicated, may hold values from 0.5 to 1.5
- w_merge: bfloat16 [4, 1408, 1408], P(None, 'col'), may hold values from -0.078125 to 0.078125
- requests: int32 [8, 16, 85], P('row'), may hold values from -1 to 511, as said below
Outputs:
- delivered: bfloat16 [8, 16, 85, 1408], P('row', 'col')
Inputs may be any that keep to these rules, and one draw needn't show every extreme that they name: `segment_ids`: ids do not fall along the tokens except to -1 for the padding at the end; every image covers a multiple of 4 tokens and starts at a multiple of 4. `recompute_rows`: the 200 offsets of one index of row are distinct. `requests`: for each index of row, the lists of all owners together name each of its 512 merged tokens exactly once; unused slots hold -1 and follow the used ones.
All inputs are finite; a program needn't handle non-finite values.
Results may differ from a plain program's by a relative error of at most 0.025.
The roundings to bfloat16 on the way count: a program that leaves them out, or rounds other values in their place, can miss the bound.
Values may be sent and summed in bfloat16 or wider, within the bound.
A program may use at most 128 MiB of HBM per device.

v0:
```python
import jax
import jax.numpy as jnp
from jax import lax
from jax.sharding import PartitionSpec as P

HD = 88
EPSILON = 1e-06
MASKED = -1e30
KEY_BLOCK = 1024


def on_device(
    hidden,
    gain_in,
    w_query,
    w_pair,
    kv_cache,
    recompute_rows,
    segment_ids,
    w_out,
    gain_merge,
    w_merge,
    requests,
):
    local_width, tok_rows = hidden.shape
    model_width = w_query.shape[1]
    n_col = model_width // local_width
    heads_here = local_width // HD
    score_scale = HD ** (-0.5)
    col_index = lax.axis_index("col")
    full_rows = lax.all_gather(hidden, "col", axis=0, tiled=True)
    out_weight = lax.all_gather(w_out, "col", axis=0, tiled=True)
    full_float = full_rows.astype(jnp.float32)
    in_mean = jnp.sum(full_float, axis=0, keepdims=True) / model_width
    in_square = jnp.sum(full_float * full_float, axis=0, keepdims=True) / model_width
    normed = (
        (full_float - in_mean)
        * lax.rsqrt(in_square - in_mean * in_mean + EPSILON)
        * gain_in.astype(jnp.float32)[:, None]
    ).astype(jnp.bfloat16)
    queries = jnp.dot(w_query, normed, preferred_element_type=jnp.float32).astype(jnp.bfloat16)
    picked_rows = recompute_rows[0]
    normed_picked = jnp.take(normed, picked_rows, axis=1)
    fresh_pairs = jnp.dot(
        w_pair.reshape(2 * local_width, model_width),
        normed_picked,
        preferred_element_type=jnp.float32,
    )
    fresh_pairs = fresh_pairs.astype(jnp.bfloat16).reshape(2, local_width, -1)
    keys_values = kv_cache.at[:, :, picked_rows].set(fresh_pairs)
    query_heads = queries.reshape(heads_here, HD, tok_rows)
    pair_local = jnp.concatenate(
        [keys_values.reshape(2 * local_width, tok_rows), segment_ids.astype(jnp.bfloat16)[None, :]],
        axis=0,
    )
    pair_all = lax.all_gather(pair_local, "row", axis=1, tiled=True)
    pair_rows = pair_all[: 2 * local_width].reshape(2, local_width, -1)
    segment_line = pair_all[2 * local_width].astype(jnp.int32)

    def take_block(carried, pair_block, segment_block):
        running_max, running_sum, weighted = carried
        key_block = pair_block[0].reshape(heads_here, HD, -1)
        value_block = pair_block[1].reshape(heads_here, HD, -1)
        scores = (
            jnp.einsum("hdq,hdk->hqk", query_heads, key_block, preferred_element_type=jnp.float32)
            * score_scale
        )
        allowed = (segment_ids[:, None] == segment_block[None, :])[None, :, :]
        new_max = jnp.maximum(running_max, jnp.max(jnp.where(allowed, scores, MASKED), axis=2))
        weights_exp = jnp.where(allowed, jnp.exp(scores - new_max[:, :, None]), 0.0)
        factor = jnp.exp(running_max - new_max)
        running_sum = running_sum * factor + jnp.sum(weights_exp, axis=2)
        product = jnp.einsum(
            "hqk,hdk->hdq",
            weights_exp.astype(jnp.bfloat16),
            value_block,
            preferred_element_type=jnp.float32,
        )
        weighted = weighted * factor[:, None, :] + product
        return (new_max, running_sum, weighted)

    starting = (
        jnp.full((heads_here, tok_rows), MASKED, jnp.float32),
        jnp.zeros((heads_here, tok_rows), jnp.float32),
        jnp.zeros((heads_here, HD, tok_rows), jnp.float32),
    )
    piece_rows = pair_rows.shape[2]
    whole_blocks = piece_rows // KEY_BLOCK

    def loop_body(block_index, loop_state):
        pair_block = lax.dynamic_slice_in_dim(pair_rows, block_index * KEY_BLOCK, KEY_BLOCK, 2)
        segment_block = lax.dynamic_slice_in_dim(
            segment_line, block_index * KEY_BLOCK, KEY_BLOCK, 0
        )
        return take_block(loop_state, pair_block, segment_block)

    running_max, running_sum, weighted = lax.fori_loop(0, whole_blocks, loop_body, starting)
    attended = (
        (weighted / running_sum[:, None, :]).astype(jnp.bfloat16).reshape(local_width, tok_rows)
    )
    chunk = tok_rows // n_col
    attended_chunk = lax.all_to_all(attended, "col", 1, 0, tiled=True)
    x_chunk = lax.dynamic_slice_in_dim(full_float, col_index * chunk, chunk, 1)
    projected = lax.dot_general(
        out_weight, attended_chunk, (((0,), (0,)), ((), ())), preferred_element_type=jnp.float32
    )
    updated = x_chunk + projected
    row_mean = jnp.sum(updated, axis=0, keepdims=True) / model_width
    row_square = jnp.sum(updated * updated, axis=0, keepdims=True) / model_width
    merger_chunk = (
        (updated - row_mean)
        * lax.rsqrt(row_square - row_mean * row_mean + EPSILON)
        * gain_merge.astype(jnp.float32)[:, None]
    ).astype(jnp.bfloat16)
    merger_in = lax.all_to_all(merger_chunk, "col", 0, 1, tiled=True)
    merged_rows = tok_rows // 4
    grouped = merger_in.reshape(local_width, merged_rows, 4)
    merged = jnp.einsum("cgi,icd->gd", grouped, w_merge, preferred_element_type=jnp.float32)
    merged_sum = lax.psum(merged.astype(jnp.bfloat16), "col")
    wanted_rows = lax.dynamic_index_in_dim(requests[0], col_index, 0, keepdims=False)
    is_valid = wanted_rows >= 0
    safe_index = jnp.where(is_valid, wanted_rows, 0)
    picked = jnp.where(is_valid[:, None], merged_sum[safe_index], jnp.zeros((), jnp.bfloat16))
    return picked.reshape(1, 1, picked.shape[0], model_width)


def solution(mesh):
    placed = (
        P("col", "row"),
        P(),
        P("col", None),
        P(None, "col", None),
        P(None, "col", "row"),
        P("row", None),
        P("row"),
        P("col", None),
        P(),
        P(None, "col", None),
        P("row", None, None),
    )
    return jax.shard_map(
        on_device,
        mesh=mesh,
        in_specs=placed,
        out_specs=P("row", "col", None, None),
        check_vma=False,
    )
```

profile of v0, /device:TPU:0, one launch (start us, length us, event | category | flops | bytes accessed | tf_op | source)
XLA Modules:
  0.0 532.2 jit_solution(17478060739190972676)
XLA Ops:
  12.5 58.2 %all-gather.4.cloned.1.call-done = bf16[1408,2048]{1,0:T(8,128)(2,1)} async-done(((bf16[88,2048]{1,0:T(8,128)(2,1)}), bf16[1408,2048]{1,0:T(8,128)(2,1)}) %all-gather.4.cloned.1.call-update) | async-done | bytes 5767184 | tf_op jit(solution)/shard_map/all_gather | solution.py:31
  70.7 8.3 %copy.31 = bf16[1408,2048]{0,1:T(8,128)(2,1)} copy(bf16[1408,2048]{1,0:T(8,128)(2,1)} %all-gather.4.cloned.1.call-done) | data formatting | bytes 11534336 | tf_op jit(solution)/shard_map/all_gather | solution.py:31
  93.1 6.9 %scatter_fusion = bf16[2,88,2048]{1,0,2:T(2,128)(2,1)S(1)} fusion(bf16[2,88,2048]{1,0,2:T(2,128)(2,1)S(1)} %copy.33, s32[200]{0:T(256)S(1)} %bitcast.125, bf16[200,2,88]{2,1,0:T(2,128)(2,1)S(1)} %bitcast.118), kind=kCustom, calls=%fused_computation.2 | custom fusion | bytes 212000 | tf_op jit(solution)/shard_map/scatter | solution.py:50
  107.2 34.4 %all-gather.6.cloned.1.call-done = bf16[177,16384]{1,0:T(8,128)(2,1)} async-done(((bf16[177,2048]{1,0:T(8,128)(2,1)}), bf16[177,16384]{1,0:T(8,128)(2,1)}) %all-gather.6.cloned.1.call-update) | async-done | bytes 5799952 | tf_op jit(solution)/shard_map/all_gather | solution.py:56
  141.7 5.8 %slice.29 = bf16[176,16384]{1,0:T(8,128)(2,1)} slice(bf16[177,16384]{1,0:T(8,128)(2,1)} %all-gather.6.cloned.1.call-done), slice={[0:176], [0:16384]} | slice | bytes 11534336 | tf_op jit(solution)/shard_map/slice | solution.py:57
  148.4 251.7 %while.18 = (s32[]{:T(128)}, f32[1,2048]{1,0:T(1,128)S(1)}, f32[1,2048]{1,0:T(1,128)S(1)}, f32[1,88,2048]{2,1,0:T(8,128)S(1)}, s32[2048]{0:T(1024)S(1)}, /*index...) while((s32[]{:T(128)}, f32[1,2048]{1,0:T(1,128)S(1)}, ...), condition=%wide.region_6.7_spmd.clone, body=%wide.region_3.0_spmd.clone.sunk | while | flops 768108544 | bytes 27504848 | solution.py:97
  148.5 5.6 %fusion.45 = (f32[2048]{0:T(1024)S(1)}, f32[1024,2048]{1,0:T(8,128)}) fusion(s32[2048]{0:T(1024)S(1)} %get-tuple-element.290, s32[1024]{0:T(1024)S(1)} %dynamic_slice.32, bf16[1,88,2048]{2,1,0:T(8,128)(2,1)S(1)} %get-tuple-element.293, bf16[2,88,16384]{2,1,0:T(8,128)(2,1)} %get-tuple-element.292, s32[]{:T(128)S(6)} %select_n.132), kind=kOutput, calls=%fused_computation.5.clone.1 | convolution fusion | flops 377485312 | bytes 8949764 | tf_op jit(solution)/shard_map/while/body/eval_jaxpr/hdq,hdk->hqk/dot_general | solution.py:65
  158.8 5.5 %fusion.49 = f32[1,88,2048]{2,1,0:T(8,128)S(1)} fusion(f32[1024,2048]{1,0:T(8,128)} %get-tuple-element.257, f32[2048]{0:T(1024)S(1)} %bitcast.110, s32[2048]{0:T(1024)S(1)} %get-tuple-element.290, s32[1024]{0:T(1024)S(1)} %dynamic_slice.32, f32[1,88,2048]{2,1,0:T(8,128)S(1)} %get-tuple-element.276, f32[2048]{0:T(1024)S(1)} %bitcast.120, ...), kind=kOutput, calls=%fused_computation.12.clone.1 | convolution fusion | flops 380125184 | bytes 10039305 | tf_op jit(solution)/shard_map/while/body/eval_jaxpr/hqk,hdk->hdq/dot_general | solution.py:73
  164.3 5.6 %fusion.45 = (f32[2048]{0:T(1024)S(1)}, f32[1024,2048]{1,0:T(8,128)}) fusion(s32[2048]{0:T(1024)S(1)} %get-tuple-element.290, s32[1024]{0:T(1024)S(1)} %dynamic_slice.32, bf16[1,88,2048]{2,1,0:T(8,128)(2,1)S(1)} %get-tuple-element.293, bf16[2,88,16384]{2,1,0:T(8,128)(2,1)} %get-tuple-element.292, s32[]{:T(128)S(6)} %select_n.132), kind=kOutput, calls=%fused_computation.5.clone.1 | convolution fusion | flops 377485312 | bytes 8949764 | tf_op jit(solution)/shard_map/while/body/eval_jaxpr/hdq,hdk->hqk/dot_general | solution.py:65
  174.5 5.4 %fusion.49 = f32[1,88,2048]{2,1,0:T(8,128)S(1)} fusion(f32[1024,2048]{1,0:T(8,128)} %get-tuple-element.257, f32[2048]{0:T(1024)S(1)} %bitcast.110, s32[2048]{0:T(1024)S(1)} %get-tuple-element.290, s32[1024]{0:T(1024)S(1)} %dynamic_slice.32, f32[1,88,2048]{2,1,0:T(8,128)S(1)} %get-tuple-element.276, f32[2048]{0:T(1024)S(1)} %bitcast.120, ...), kind=kOutput, calls=%fused_computation.12.clone.1 | convolution fusion | flops 380125184 | bytes 10039305 | tf_op jit(solution)/shard_map/while/body/eval_jaxpr/hqk,hdk->hdq/dot_general | solution.py:73
  180.0 5.6 %fusion.45 = (f32[2048]{0:T(1024)S(1)}, f32[1024,2048]{1,0:T(8,128)}) fusion(s32[2048]{0:T(1024)S(1)} %get-tuple-element.290, s32[1024]{0:T(1024)S(1)} %dynamic_slice.32, bf16[1,88,2048]{2,1,0:T(8,128)(2,1)S(1)} %get-tuple-element.293, bf16[2,88,16384]{2,1,0:T(8,128)(2,1)} %get-tuple-element.292, s32[]{:T(128)S(6)} %select_n.132), kind=kOutput, calls=%fused_computation.5.clone.1 | convolution fusion | flops 377485312 | bytes 8949764 | tf_op jit(solution)/shard_map/while/body/eval_jaxpr/hdq,hdk->hqk/dot_general | solution.py:65
  195.9 5.6 %fusion.45 = (f32[2048]{0:T(1024)S(1)}, f32[1024,2048]{1,0:T(8,128)}) fusion(s32[2048]{0:T(1024)S(1)} %get-tuple-element.290, s32[1024]{0:T(1024)S(1)} %dynamic_slice.32, bf16[1,88,2048]{2,1,0:T(8,128)(2,1)S(1)} %get-tuple-element.293, bf16[2,88,16384]{2,1,0:T(8,128)(2,1)} %get-tuple-element.292, s32[]{:T(128)S(6)} %select_n.132), kind=kOutput, calls=%fused_computation.5.clone.1 | convolution fusion | flops 377485312 | bytes 8949764 | tf_op jit(solution)/shard_map/while/body/eval_jaxpr/hdq,hdk->hqk/dot_general | solution.py:65
  211.6 5.6 %fusion.45 = (f32[2048]{0:T(1024)S(1)}, f32[1024,2048]{1,0:T(8,128)}) fusion(s32[2048]{0:T(1024)S(1)} %get-tuple-element.290, s32[1024]{0:T(1024)S(1)} %dynamic_slice.32, bf16[1,88,2048]{2,1,0:T(8,128)(2,1)S(1)} %get-tuple-element.293, bf16[2,88,16384]{2,1,0:T(8,128)(2,1)} %get-tuple-element.292, s32[]{:T(128)S(6)} %select_n.132), kind=kOutput, calls=%fused_computation.5.clone.1 | convolution fusion | flops 377485312 | bytes 8949764 | tf_op jit(solution)/shard_map/while/body/eval_jaxpr/hdq,hdk->hqk/dot_general | solution.py:65
  227.3 5.6 %fusion.45 = (f32[2048]{0:T(1024)S(1)}, f32[1024,2048]{1,0:T(8,128)}) fusion(s32[2048]{0:T(1024)S(1)} %get-tuple-element.290, s32[1024]{0:T(1024)S(1)} %dynamic_slice.32, bf16[1,88,2048]{2,1,0:T(8,128)(2,1)S(1)} %get-tuple-element.293, bf16[2,88,16384]{2,1,0:T(8,128)(2,1)} %get-tuple-element.292, s32[]{:T(128)S(6)} %select_n.132), kind=kOutput, calls=%fused_computation.5.clone.1 | convolution fusion | flops 377485312 | bytes 8949764 | tf_op jit(solution)/shard_map/while/body/eval_jaxpr/hdq,hdk->hqk/dot_general | solution.py:65
  237.6 5.4 %fusion.49 = f32[1,88,2048]{2,1,0:T(8,128)S(1)} fusion(f32[1024,2048]{1,0:T(8,128)} %get-tuple-element.257, f32[2048]{0:T(1024)S(1)} %bitcast.110, s32[2048]{0:T(1024)S(1)} %get-tuple-element.290, s32[1024]{0:T(1024)S(1)} %dynamic_slice.32, f32[1,88,2048]{2,1,0:T(8,128)S(1)} %get-tuple-element.276, f32[2048]{0:T(1024)S(1)} %bitcast.120, ...), kind=kOutput, calls=%fused_computation.12.clone.1 | convolution fusion | flops 380125184 | bytes 10039305 | tf_op jit(solution)/shard_map/while/body/eval_jaxpr/hqk,hdk->hdq/dot_general | solution.py:73
  243.0 5.6 %fusion.45 = (f32[2048]{0:T(1024)S(1)}, f32[1024,2048]{1,0:T(8,128)}) fusion(s32[2048]{0:T(1024)S(1)} %get-tuple-element.290, s32[1024]{0:T(1024)S(1)} %dynamic_slice.32, bf16[1,88,2048]{2,1,0:T(8,128)(2,1)S(1)} %get-tuple-element.293, bf16[2,88,16384]{2,1,0:T(8,128)(2,1)} %get-tuple-element.292, s32[]{:T(128)S(6)} %select_n.132), kind=kOutput, calls=%fused_computation.5.clone.1 | convolution fusion | flops 377485312 | bytes 8949764 | tf_op jit(solution)/shard_map/while/body/eval_jaxpr/hdq,hdk->hqk/dot_general | solution.py:65
  253.3 5.4 %fusion.49 = f32[1,88,2048]{2,1,0:T(8,128)S(1)} fusion(f32[1024,2048]{1,0:T(8,128)} %get-tuple-element.257, f32[2048]{0:T(1024)S(1)} %bitcast.110, s32[2048]{0:T(1024)S(1)} %get-tuple-element.290, s32[1024]{0:T(1024)S(1)} %dynamic_slice.32, f32[1,88,2048]{2,1,0:T(8,128)S(1)} %get-tuple-element.276, f32[2048]{0:T(1024)S(1)} %bitcast.120, ...), kind=kOutput, calls=%fused_computation.12.clone.1 | convolution fusion | flops 380125184 | bytes 10039305 | tf_op jit(solution)/shard_map/while/body/eval_jaxpr/hqk,hdk->hdq/dot_general | solution.py:73
  258.7 5.6 %fusion.45 = (f32[2048]{0:T(1024)S(1)}, f32[1024,2048]{1,0:T(8,128)}) fusion(s32[2048]{0:T(1024)S(1)} %get-tuple-element.290, s32[1024]{0:T(1024)S(1)} %dynamic_slice.32, bf16[1,88,2048]{2,1,0:T(8,128)(2,1)S(1)} %get-tuple-element.293, bf16[2,88,16384]{2,1,0:T(8,128)(2,1)} %get-tuple-element.292, s32[]{:T(128)S(6)} %select_n.132), kind=kOutput, calls=%fused_computation.5.clone.1 | convolution fusion | flops 377485312 | bytes 8949764 | tf_op jit(solution)/shard_map/while/body/eval_jaxpr/hdq,hdk->hqk/dot_general | solution.py:65
  274.4 5.6 %fusion.45 = (f32[2048]{0:T(1024)S(1)}, f32[1024,2048]{1,0:T(8,128)}) fusion(s32[2048]{0:T(1024)S(1)} %get-tuple-element.290, s32[1024]{0:T(1024)S(1)} %dynamic_slice.32, bf16[1,88,2048]{2,1,0:T(8,128)(2,1)S(1)} %get-tuple-element.293, bf16[2,88,16384]{2,1,0:T(8,128)(2,1)} %get-tuple-element.292, s32[]{:T(128)S(6)} %select_n.132), kind=kOutput, calls=%fused_computation.5.clone.1 | convolution fusion | flops 377485312 | bytes 8949764 | tf_op jit(solution)/shard_map/while/body/eval_jaxpr/hdq,hdk->hqk/dot_general | solution.py:65
  290.2 5.6 %fusion.45 = (f32[2048]{0:T(1024)S(1)}, f32[1024,2048]{1,0:T(8,128)}) fusion(s32[2048]{0:T(1024)S(1)} %get-tuple-element.290, s32[1024]{0:T(1024)S(1)} %dynamic_slice.32, bf16[1,88,2048]{2,1,0:T(8,128)(2,1)S(1)} %get-tuple-element.293, bf16[2,88,16384]{2,1,0:T(8,128)(2,1)} %get-tuple-element.292, s32[]{:T(128)S(6)} %select_n.132), kind=kOutput, calls=%fused_computation.5.clone.1 | convolution fusion | flops 377485312 | bytes 8949764 | tf_op jit(solution)/shard_map/while/body/eval_jaxpr/hdq,hdk->hqk/dot_general | solution.py:65
  305.9 5.6 %fusion.45 = (f32[2048]{0:T(1024)S(1)}, f32[1024,2048]{1,0:T(8,128)}) fusion(s32[2048]{0:T(1024)S(1)} %get-tuple-element.290, s32[1024]{0:T(1024)S(1)} %dynamic_slice.32, bf16[1,88,2048]{2,1,0:T(8,128)(2,1)S(1)} %get-tuple-element.293, bf16[2,88,16384]{2,1,0:T(8,128)(2,1)} %get-tuple-element.292, s32[]{:T(128)S(6)} %select_n.132), kind=kOutput, calls=%fused_computation.5.clone.1 | convolution fusion | flops 377485312 | bytes 8949764 | tf_op jit(solution)/shard_map/while/body/eval_jaxpr/hdq,hdk->hqk/dot_general | solution.py:65
  316.1 5.4 %fusion.49 = f32[1,88,2048]{2,1,0:T(8,128)S(1)} fusion(f32[1024,2048]{1,0:T(8,128)} %get-tuple-element.257, f32[2048]{0:T(1024)S(1)} %bitcast.110, s32[2048]{0:T(1024)S(1)} %get-tuple-element.290, s32[1024]{0:T(1024)S(1)} %dynamic_slice.32, f32[1,88,2048]{2,1,0:T(8,128)S(1)} %get-tuple-element.276, f32[2048]{0:T(1024)S(1)} %bitcast.120, ...), kind=kOutput, calls=%fused_computation.12.clone.1 | convolution fusion | flops 380125184 | bytes 10039305 | tf_op jit(solution)/shard_map/while/body/eval_jaxpr/hqk,hdk->hdq/dot_general | solution.py:73
  321.6 5.6 %fusion.45 = (f32[2048]{0:T(1024)S(1)}, f32[1024,2048]{1,0:T(8,128)}) fusion(s32[2048]{0:T(1024)S(1)} %get-tuple-element.290, s32[1024]{0:T(1024)S(1)} %dynamic_slice.32, bf16[1,88,2048]{2,1,0:T(8,128)(2,1)S(1)} %get-tuple-element.293, bf16[2,88,16384]{2,1,0:T(8,128)(2,1)} %get-tuple-element.292, s32[]{:T(128)S(6)} %select_n.132), kind=kOutput, calls=%fused_computation.5.clone.1 | convolution fusion | flops 377485312 | bytes 8949764 | tf_op jit(solution)/shard_map/while/body/eval_jaxpr/hdq,hdk->hqk/dot_general | solution.py:65
  331.8 5.4 %fusion.49 = f32[1,88,2048]{2,1,0:T(8,128)S(1)} fusion(f32[1024,2048]{1,0:T(8,128)} %get-tuple-element.257, f32[2048]{0:T(1024)S(1)} %bitcast.110, s32[2048]{0:T(1024)S(1)} %get-tuple-element.290, s32[1024]{0:T(1024)S(1)} %dynamic_slice.32, f32[1,88,2048]{2,1,0:T(8,128)S(1)} %get-tuple-element.276, f32[2048]{0:T(1024)S(1)} %bitcast.120, ...), kind=kOutput, calls=%fused_computation.12.clone.1 | convolution fusion | flops 380125184 | bytes 10039305 | tf_op jit(solution)/shard_map/while/body/eval_jaxpr/hqk,hdk->hdq/dot_general | solution.py:73
  337.3 5.6 %fusion.45 = (f32[2048]{0:T(1024)S(1)}, f32[1024,2048]{1,0:T(8,128)}) fusion(s32[2048]{0:T(1024)S(1)} %get-tuple-element.290, s32[1024]{0:T(1024)S(1)} %dynamic_slice.32, bf16[1,88,2048]{2,1,0:T(8,128)(2,1)S(1)} %get-tuple-element.293, bf16[2,88,16384]{2,1,0:T(8,128)(2,1)} %get-tuple-element.292, s32[]{:T(128)S(6)} %select_n.132), kind=kOutput, calls=%fused_computation.5.clone.1 | convolution fusion | flops 377485312 | bytes 8949764 | tf_op jit(solution)/shard_map/while/body/eval_jaxpr/hdq,hdk->hqk/dot_general | solution.py:65
  353.0 5.6 %fusion.45 = (f32[2048]{0:T(1024)S(1)}, f32[1024,2048]{1,0:T(8,128)}) fusion(s32[2048]{0:T(1024)S(1)} %get-tuple-element.290, s32[1024]{0:T(1024)S(1)} %dynamic_slice.32, bf16[1,88,2048]{2,1,0:T(8,128)(2,1)S(1)} %get-tuple-element.293, bf16[2,88,16384]{2,1,0:T(8,128)(2,1)} %get-tuple-element.292, s32[]{:T(128)S(6)} %select_n.132), kind=kOutput, calls=%fused_computation.5.clone.1 | convolution fusion | flops 377485312 | bytes 8949764 | tf_op jit(solution)/shard_map/while/body/eval_jaxpr/hdq,hdk->hqk/dot_general | solution.py:65
  368.7 5.6 %fusion.45 = (f32[2048]{0:T(1024)S(1)}, f32[1024,2048]{1,0:T(8,128)}) fusion(s32[2048]{0:T(1024)S(1)} %get-tuple-element.290, s32[1024]{0:T(1024)S(1)} %dynamic_slice.32, bf16[1,88,2048]{2,1,0:T(8,128)(2,1)S(1)} %get-tuple-element.293, bf16[2,88,16384]{2,1,0:T(8,128)(2,1)} %get-tuple-element.292, s32[]{:T(128)S(6)} %select_n.132), kind=kOutput, calls=%fused_computation.5.clone.1 | convolution fusion | flops 377485312 | bytes 8949764 | tf_op jit(solution)/shard_map/while/body/eval_jaxpr/hdq,hdk->hqk/dot_general | solution.py:65
  384.4 5.6 %fusion.45 = (f32[2048]{0:T(1024)S(1)}, f32[1024,2048]{1,0:T(8,128)}) fusion(s32[2048]{0:T(1024)S(1)} %get-tuple-element.290, s32[1024]{0:T(1024)S(1)} %dynamic_slice.32, bf16[1,88,2048]{2,1,0:T(8,128)(2,1)S(1)} %get-tuple-element.293, bf16[2,88,16384]{2,1,0:T(8,128)(2,1)} %get-tuple-element.292, s32[]{:T(128)S(6)} %select_n.132), kind=kOutput, calls=%fused_computation.5.clone.1 | convolution fusion | flops 377485312 | bytes 8949764 | tf_op jit(solution)/shard_map/while/body/eval_jaxpr/hdq,hdk->hqk/dot_general | solution.py:65
  401.1 6.9 %all-to-all-start = ((bf16[88,16,128]{2,0,1:T(8,128)(2,1)}), bf16[88,16,128]{2,0,1:T(8,128)(2,1)S(1)}, u32[]{:S(2)}, u32[]{:S(2)}) async-start(bf16[88,16,128]{2,0,1:T(8,128)(2,1)} %copy.35), calls=%async_computation | async-start | bytes 720896 | tf_op jit(solution)/shard_map/all_to_all | solution.py:102
  408.1 7.6 %convert_element_type.50 = f32[1408,2048]{0,1:T(8,128)} convert(bf16[1408,2048]{0,1:T(8,128)(2,1)} %copy.31) | non-fusion elementwise | flops 2883584 | bytes 17301504 | tf_op jit(solution)/shard_map/convert_element_type | solution.py:33
  421.7 14.1 %all_to_all.35 = bf16[16,88,128]{2,1,0:T(8,128)(2,1)S(1)} all-to-all(bf16[16,88,128]{2,1,0:T(8,128)(2,1)S(1)} %bitcast.114), channel_id=1, replica_groups=mesh['row'=8,'col'=16] {'col'}, dimensions={0} | all-to-all | bytes 720896 | tf_op jit(solution)/shard_map/all_to_all | solution.py:115
  439.6 82.8 %all-reduce.2.cloned.1.call-done = bf16[512,1408]{1,0:T(8,128)(2,1)} async-done(((bf16[512,1408]{1,0:T(8,128)(2,1)}), bf16[512,1408]{1,0:T(8,128)(2,1)}) %all-reduce.2.cloned.1.call-update) | async-done | bytes 1441808 | tf_op jit(solution)/shard_map/psum | solution.py:119
  (147 shorter events, 170.8 us)
Async XLA Ops:
  6.5 429.6 %copy-start = (bf16[4,88,1408]{2,1,0:T(8,128)(2,1)S(1)}, bf16[4,88,1408]{2,1,0:T(8,128)(2,1)}, u32[]{:S(2)}) copy-start(bf16[4,88,1408]{2,1,0:T(8,128)(2,1)} %param.22) | copy-start | bytes 2973700
  6.5 64.2 %all-gather.4.cloned.1.call-start = ((), (), s32[]{:S(2)}) async-start(), calls=%async_computation.2 | async-start | bytes 6127616 | tf_op jit(solution)/shard_map/all_gather | solution.py:31
  7.3 134.4 %all-gather.6.cloned.1.call-start = ((), (), s32[]{:S(2)}) async-start(), calls=%async_computation.3 | async-start | bytes 6782976 | tf_op jit(solution)/shard_map/all_gather | solution.py:56
  79.1 4.5 copy-start.1
  83.6 9.0 %copy-start.5 = (bf16[2,88,1408]{2,1,0:T(8,128)(2,1)S(1)}, bf16[2,88,1408]{2,1,0:T(8,128)(2,1)}, u32[]{:S(2)}) copy-start(bf16[2,88,1408]{2,1,0:T(8,128)(2,1)} %param.16) | copy-start | bytes 1486852
  87.5 15.0 %copy-start.3 = (bf16[88,1408]{1,0:T(8,128)(2,1)S(1)}, bf16[88,1408]{1,0:T(8,128)(2,1)}, u32[]{:S(2)}) copy-start(bf16[88,1408]{1,0:T(8,128)(2,1)} %param.15) | copy-start | bytes 743428
  101.8 313.8 %all-gather.8.cloned.1.call-start = ((), (), s32[]{:S(2)}) async-start(), calls=%async_computation.4 | async-start | bytes 4212736 | tf_op jit(solution)/shard_map/all_gather | solution.py:32
  102.5 45.9 %copy-start.2 = (s32[2048]{0:T(1024)S(1)}, s32[2048]{0:T(1024)}, u32[]{:S(2)}) copy-start(s32[2048]{0:T(1024)} %param.19) | copy-start | bytes 24580
  148.4 259.6 %copy-start.4 = (bf16[1408]{0:T(1024)(128)(2,1)S(1)}, bf16[1408]{0:T(1024)(128)(2,1)}, u32[]{:S(2)}) copy-start(bf16[1408]{0:T(1024)(128)(2,1)} %param.21) | copy-start | bytes 8452
  401.1 17.0 %all-to-all-start = ((bf16[88,16,128]{2,0,1:T(8,128)(2,1)}), bf16[88,16,128]{2,0,1:T(8,128)(2,1)S(1)}, u32[]{:S(2)}, u32[]{:S(2)}) async-start(bf16[88,16,128]{2,0,1:T(8,128)(2,1)} %copy.35), calls=%async_computation | async-start | bytes 720896 | tf_op jit(solution)/shard_map/all_to_all | solution.py:102
  408.0 114.4 %all-reduce.2.cloned.1.call-start = ((), (), s32[]{:S(2)}) async-start(), calls=%async_computation.5 | async-start | bytes 2883584 | tf_op jit(solution)/shard_map/psum | solution.py:119
Sparse Core Ops, SparseCore 0:
  9.5 61.1 all-gather.3
  101.9 39.7 all-gather.5
  143.8 50.4 all-gather.7
  438.4 83.9 all-reduce.1
where the time goes:
time: 534 us; the launch traced here: 532 us
  matrix products  187 us (35%)
  waiting for transfers between devices  179 us (34%)
  other arithmetic  97.5 us (18%)
  local copies, waits for them, and re-layouts  33.4 us (6%)
  blocking collectives  14.1 us (3%)
  between operations  13.4 us (3%)
  starting transfers between devices  7.17 us (1%)
    dot_general x16, matrix products, take_block(): jnp.einsum('hdq,hdk->hqk', query_heads, key_block, preferred_element_type...  89.9 us
    dot_general x16, matrix products, take_block(): jnp.einsum('hqk,hdk->hdq', weights_exp.astype(jnp.bfloat16), value_block,...  86.4 us
    psum x1, waiting for transfers between devices, on_device(): merged_sum = lax.psum(merged.astype(jnp.bfloat16), 'col')  82.8 us
    reduce_sum x16, other arithmetic, take_block(): running_sum = running_sum * factor + jnp.sum(weights_exp, axis=2)  73.4 us
    all_gather x1, waiting for transfers between devices, on_device(): full_rows = lax.all_gather(hidden, 'col', axis=0, tiled=True)  58.2 us
    all_gather x1, waiting for transfers between devices, on_device(): pair_all = lax.all_gather(pair_local, 'row', axis=1, tiled=True)  34.4 us
    all_to_all x1, blocking collectives, on_device(): merger_in = lax.all_to_all(merger_chunk, 'col', 0, 1, tiled=True)  14.1 us
  transfers between devices with their start and end apart: 5, of which 4 were waited for; matrix products, arithmetic and copies ran while one was open for 52% of the time, Pallas kernels for 0%

commit v1 on v0

--- a/solution.py
+++ b/solution.py
@@ -116,7 +116,7 @@
     merged_rows = tok_rows // 4
     grouped = merger_in.reshape(local_width, merged_rows, 4)
     merged = jnp.einsum("cgi,icd->gd", grouped, w_merge, preferred_element_type=jnp.float32)
-    merged_sum = lax.psum(merged.astype(jnp.bfloat16), "col")
+    merged_sum = jnp.sum(lax.all_gather(merged.astype(jnp.bfloat16), "col"), axis=0)
     wanted_rows = lax.dynamic_index_in_dim(requests[0], col_index, 0, keepdims=False)
     is_valid = wanted_rows >= 0
     safe_index = jnp.where(is_valid, wanted_rows, 0)

time: 534 us -> 601 us (1.13)
  waiting for transfers between devices: 179 us -> 235 us
  other arithmetic: 97.5 us -> 110 us
    all_gather x0 -> x1, waiting for transfers between devices: none -> 139 us  [on_device(): lax.all_gather(merged.astype(jnp.bfloat16), 'col')]
    psum x1 -> x0, waiting for transfers between devices: 82.8 us -> none  [on_device(): merged_sum = lax.psum(merged.astype(jnp.bfloat16), 'col')]
    reduce_sum x0 -> x1, other arithmetic: none -> 12.2 us  [on_device(): jnp.sum(lax.all_gather(merged.astype(jnp.bfloat16), 'col'), axis=0)]
  transfers between devices with their start and end apart: 5 -> 5, of which waited for: 4 -> 4; matrix products, arithmetic and copies ran while one was open for 52% -> 46% of each run, Pallas kernels for 0% -> 0%
where the time goes in v1:
time: 601 us; the launch traced here: 599 us
  waiting for transfers between devices  235 us (39%)
  matrix products  187 us (31%)
  other arithmetic  110 us (18%)
  local copies, waits for them, and re-layouts  31.7 us (5%)
  blocking collectives  14.1 us (2%)
  between operations  13.4 us (2%)
  starting transfers between devices  7.17 us (1%)
    all_gather x1, waiting for transfers between devices, on_device(): lax.all_gather(merged.astype(jnp.bfloat16), 'col')  139 us
    dot_general x16, matrix products, take_block(): jnp.einsum('hdq,hdk->hqk', query_heads, key_block, preferred_element_type...  89.9 us
    dot_general x16, matrix products, take_block(): jnp.einsum('hqk,hdk->hdq', weights_exp.astype(jnp.bfloat16), value_block,...  86.4 us
    reduce_sum x16, other arithmetic, take_block(): running_sum = running_sum * factor + jnp.sum(weights_exp, axis=2)  73.4 us
    all_gather x1, waiting for transfers between devices, on_device(): full_rows = lax.all_gather(hidden, 'col', axis=0, tiled=True)  58.2 us
    all_gather x1, waiting for transfers between devices, on_device(): pair_all = lax.all_gather(pair_local, 'row', axis=1, tiled=True)  34.4 us
    all_to_all x1, blocking collectives, on_device(): merger_in = lax.all_to_all(merger_chunk, 'col', 0, 1, tiled=True)  14.1 us
    reduce_sum x1, other arithmetic, on_device(): jnp.sum(lax.all_gather(merged.astype(jnp.bfloat16), 'col'), axis=0)  12.2 us
  transfers between devices with their start and end apart: 5, of which 4 were waited for; matrix products, arithmetic and copies ran while one was open for 46% of the time, Pallas kernels for 0%

profile of v1, /device:TPU:0, one launch (start us, length us, event | category | flops | bytes accessed | tf_op | source)
XLA Modules:
  0.0 598.6 jit_solution(9178307829313079656)
XLA Ops:
  12.5 58.2 %all-gather.6.cloned.1.call-done = bf16[1408,2048]{1,0:T(8,128)(2,1)} async-done(((bf16[88,2048]{1,0:T(8,128)(2,1)}), bf16[1408,2048]{1,0:T(8,128)(2,1)}) %all-gather.6.cloned.1.call-update) | async-done | bytes 5767184 | tf_op jit(solution)/shard_map/all_gather | solution.py:31
  70.7 8.3 %copy.31 = bf16[1408,2048]{0,1:T(8,128)(2,1)} copy(bf16[1408,2048]{1,0:T(8,128)(2,1)} %all-gather.6.cloned.1.call-done) | data formatting | bytes 11534336 | tf_op jit(solution)/shard_map/all_gather | solution.py:31
  93.1 6.9 %scatter_fusion = bf16[2,88,2048]{1,0,2:T(2,128)(2,1)S(1)} fusion(bf16[2,88,2048]{1,0,2:T(2,128)(2,1)S(1)} %copy.33, s32[200]{0:T(256)S(1)} %bitcast.127, bf16[200,2,88]{2,1,0:T(2,128)(2,1)S(1)} %bitcast.120), kind=kCustom, calls=%fused_computation.2 | custom fusion | bytes 212000 | tf_op jit(solution)/shard_map/scatter | solution.py:50
  107.2 34.4 %all-gather.8.cloned.1.call-done = bf16[177,16384]{1,0:T(8,128)(2,1)} async-done(((bf16[177,2048]{1,0:T(8,128)(2,1)}), bf16[177,16384]{1,0:T(8,128)(2,1)}) %all-gather.8.cloned.1.call-update) | async-done | bytes 5799952 | tf_op jit(solution)/shard_map/all_gather | solution.py:56
  141.7 5.8 slice.29
  148.4 251.7 %while.18 = (s32[]{:T(128)}, f32[1,2048]{1,0:T(1,128)S(1)}, f32[1,2048]{1,0:T(1,128)S(1)}, f32[1,88,2048]{2,1,0:T(8,128)S(1)}, s32[2048]{0:T(1024)S(1)}, /*index...) while((s32[]{:T(128)}, f32[1,2048]{1,0:T(1,128)S(1)}, ...), condition=%wide.region_6.7_spmd.clone, body=%wide.region_3.0_spmd.clone.sunk | while | flops 768108544 | bytes 27504848 | solution.py:97
  148.5 5.6 fusion.45
  158.8 5.5 fusion.49
  164.3 5.6 fusion.45
  174.5 5.4 fusion.49
  180.0 5.6 fusion.45
  195.9 5.6 fusion.45
  211.6 5.6 fusion.45
  227.3 5.6 fusion.45
  237.6 5.4 fusion.49
  243.0 5.6 fusion.45
  253.3 5.4 fusion.49
  258.7 5.6 fusion.45
  274.4 5.6 fusion.45
  290.2 5.6 fusion.45
  305.9 5.6 fusion.45
  316.1 5.4 fusion.49
  321.6 5.6 fusion.45
  337.3 5.6 fusion.45
  353.0 5.6 fusion.45
  368.7 5.6 fusion.45
  384.4 5.6 fusion.45
  401.1 6.9 %all-to-all-start = ((bf16[88,16,128]{2,0,1:T(8,128)(2,1)}), bf16[88,16,128]{2,0,1:T(8,128)(2,1)S(1)}, u32[]{:S(2)}, u32[]{:S(2)}) async-start(bf16[88,16,128]{2,0,1:T(8,128)(2,1)} %copy.35), calls=%async_computation | async-start | bytes 720896 | tf_op jit(solution)/shard_map/all_to_all | solution.py:102
  408.1 7.6 %convert_element_type.52 = f32[1408,2048]{0,1:T(8,128)} convert(bf16[1408,2048]{0,1:T(8,128)(2,1)} %copy.31) | non-fusion elementwise | flops 2883584 | bytes 17301504 | tf_op jit(solution)/shard_map/convert_element_type | solution.py:33
  421.7 14.1 %all_to_all.35 = bf16[16,88,128]{2,1,0:T(8,128)(2,1)S(1)} all-to-all(bf16[16,88,128]{2,1,0:T(8,128)(2,1)S(1)} %bitcast.116), channel_id=1, replica_groups=mesh['row'=8,'col'=16] {'col'}, dimensions={0} | all-to-all | bytes 720896 | tf_op jit(solution)/shard_map/all_to_all | solution.py:115
  439.6 138.7 %all-gather.12.cloned.1.call-done = bf16[8192,1408]{1,0:T(8,128)(2,1)} async-done(((bf16[512,1408]{1,0:T(8,128)(2,1)}), bf16[8192,1408]{1,0:T(8,128)(2,1)}) %all-gather.12.cloned.1.call-update) | async-done | bytes 23068688 | tf_op jit(solution)/shard_map/all_gather | solution.py:119
  578.3 12.2 %reduce_sum.65 = bf16[512,1408]{1,0:T(8,128)(2,1)S(1)} reduce(bf16[16,512,1408]{2,1,0:T(8,128)(2,1)} %bitcast.109, bf16[]{:T(256)} %constant.104.clone.1), dimensions={0}, to_apply=%region_9.10 | reduce | flops 10813440 | bytes 24510466 | tf_op jit(solution)/shard_map/reduce_sum | solution.py:119
  (148 shorter events, 174.4 us)
Async XLA Ops:
  6.5 429.6 %copy-start = (bf16[4,88,1408]{2,1,0:T(8,128)(2,1)S(1)}, bf16[4,88,1408]{2,1,0:T(8,128)(2,1)}, u32[]{:S(2)}) copy-start(bf16[4,88,1408]{2,1,0:T(8,128)(2,1)} %param.22) | copy-start | bytes 2973700
  6.5 64.2 %all-gather.6.cloned.1.call-start = ((), (), s32[]{:S(2)}) async-start(), calls=%async_computation.2 | async-start | bytes 6127616 | tf_op jit(solution)/shard_map/all_gather | solution.py:31
  7.3 134.4 %all-gather.8.cloned.1.call-start = ((), (), s32[]{:S(2)}) async-start(), calls=%async_computation.3 | async-start | bytes 6782976 | tf_op jit(solution)/shard_map/all_gather | solution.py:56
  79.1 4.5 copy-start.1
  83.6 9.0 %copy-start.5 = (bf16[2,88,1408]{2,1,0:T(8,128)(2,1)S(1)}, bf16[2,88,1408]{2,1,0:T(8,128)(2,1)}, u32[]{:S(2)}) copy-start(bf16[2,88,1408]{2,1,0:T(8,128)(2,1)} %param.16) | copy-start | bytes 1486852
  87.5 15.0 %copy-start.3 = (bf16[88,1408]{1,0:T(8,128)(2,1)S(1)}, bf16[88,1408]{1,0:T(8,128)(2,1)}, u32[]{:S(2)}) copy-start(bf16[88,1408]{1,0:T(8,128)(2,1)} %param.15) | copy-start | bytes 743428
  101.8 313.8 %all-gather.10.cloned.1.call-start = ((), (), s32[]{:S(2)}) async-start(), calls=%async_computation.4 | async-start | bytes 4212736 | tf_op jit(solution)/shard_map/all_gather | solution.py:32
  102.5 45.9 %copy-start.2 = (s32[2048]{0:T(1024)S(1)}, s32[2048]{0:T(1024)}, u32[]{:S(2)}) copy-start(s32[2048]{0:T(1024)} %param.19) | copy-start | bytes 24580
  148.4 259.6 %copy-start.4 = (bf16[1408]{0:T(1024)(128)(2,1)S(1)}, bf16[1408]{0:T(1024)(128)(2,1)}, u32[]{:S(2)}) copy-start(bf16[1408]{0:T(1024)(128)(2,1)} %param.21) | copy-start | bytes 8452
  401.1 17.0 %all-to-all-start = ((bf16[88,16,128]{2,0,1:T(8,128)(2,1)}), bf16[88,16,128]{2,0,1:T(8,128)(2,1)S(1)}, u32[]{:S(2)}, u32[]{:S(2)}) async-start(bf16[88,16,128]{2,0,1:T(8,128)(2,1)} %copy.35), calls=%async_computation | async-start | bytes 720896 | tf_op jit(solution)/shard_map/all_to_all | solution.py:102
  408.0 170.4 %all-gather.12.cloned.1.call-start = ((), (), s32[]{:S(2)}) async-start(), calls=%async_computation.5 | async-start | bytes 24510464 | tf_op jit(solution)/shard_map/all_gather | solution.py:119
Sparse Core Ops, SparseCore 0:
  9.5 61.1 all-gather.5
  101.9 39.7 all-gather.7
  143.8 50.4 all-gather.9
  438.4 139.9 all-gather.11
